TPU v7x, 32 devices: a whole 2x2x4 slice. The times are simulated.
32 devices in a mesh: section: 4 (over y, x), row: 2 (over core), col: 4 (over z).
Axes of the slice: x: 2, y: 2, z: 4, core: 2. Of those that a mesh axis runs over, the one named last changes fastest.
Arguments:
- features: bfloat16 [2, 2, 8, 64, 192], P(None, None, 'row', 'col'), may hold values from -6 to 6
- gate_weight: bfloat16 [4, 3456, 768], P('section', 'row'), may hold values from -0.109375 to 0.109375
- gate_bias: float32 [4, 768], P('section'), may hold values from -3 to 3
Outputs:
- level_hidden: bfloat16 [4, 2, 2, 8, 64, 192], P('section', None, None, 'row', 'col')
All inputs are finite; a program needn't handle non-finite values.
Results may differ from a plain program's by a relative error of at most 0.005.
Values may be sent and summed in bfloat16 or wider, within the bound.
No kernel may reach another device: no remote copies, remote signals or barrier semaphores. Data moves between devices by JAX's collectives and lax.ppermute only.
A program may use at most 64 MiB of HBM per device.

v0:
```python
import jax
import jax.numpy as jnp
from jax import lax
from jax.sharding import PartitionSpec as P


def with_halo(array, sides, width):
    for axis, dim in sides:
        size, length = (lax.axis_size(axis), array.shape[dim])
        up = [(i, (i + 1) % size) for i in range(size - 1)]
        down = [(j, i) for i, j in up]
        last = lax.slice_in_dim(array, length - width, length, axis=dim)
        first = lax.slice_in_dim(array, 0, width, axis=dim)
        before = lax.ppermute(last, axis, up)
        after = lax.ppermute(first, axis, down)
        array = jnp.concatenate([before, array, after], axis=dim)
    return array


def shortened(array):

    def short(part):
        return part.astype(jnp.bfloat16) if part.dtype == jnp.float32 else part

    return jax.tree.map(short, array)


def from_behind(block, axis, distance):
    devices = range(lax.axis_size(axis))
    route = [(i - distance, i) for i in devices if i - distance in devices]
    return lax.ppermute(block, axis, route)


def cell_update(gate_values, memory, channels):
    in_gate = jax.nn.sigmoid(gate_values[:, :channels])
    forget = jax.nn.sigmoid(gate_values[:, channels : 2 * channels])
    candidate = jnp.tanh(gate_values[:, 2 * channels : 3 * channels])
    out_gate = jax.nn.sigmoid(gate_values[:, 3 * channels :])
    next_memory = forget * memory + in_gate * candidate
    next_hidden = (out_gate * jnp.tanh(next_memory)).astype(jnp.bfloat16)
    return (next_hidden, next_memory)


def make_patches(padded, tile_rows, tile_cols):
    tap_list = []
    for row_tap in range(3):
        for col_tap in range(3):
            tap_list.append(
                padded[:, row_tap : row_tap + tile_rows, col_tap : col_tap + tile_cols, :]
            )
    joined = jnp.concatenate(tap_list, axis=-1)
    return joined.reshape(-1, joined.shape[-1])


def local(features, gate_weight, gate_bias):
    batch_size, frame_count, tile_rows, tile_cols, channels = features.shape
    group_count = 1
    group_rows = batch_size // group_count
    section_index = lax.axis_index("section")
    start_moment = section_index + (section_index >= 2).astype(jnp.int32)
    layer_bias = gate_bias[0]
    half_shape = (group_rows, tile_rows, tile_cols, channels)
    full_shape = (batch_size, tile_rows, tile_cols, channels)
    own_hidden = jnp.zeros(full_shape, jnp.bfloat16)
    own_memory = jnp.zeros(full_shape, jnp.float32)
    held_hidden = jnp.zeros(full_shape, jnp.bfloat16)
    held_memory = jnp.zeros(full_shape, jnp.float32)
    recorded = jnp.zeros((batch_size, frame_count, tile_rows, tile_cols, channels), jnp.bfloat16)
    recv_hidden = jnp.zeros(half_shape, jnp.bfloat16)
    recv_memory = jnp.zeros(half_shape, jnp.float32)
    context = jnp.zeros(half_shape, jnp.bfloat16)
    zero_hidden = jnp.zeros(half_shape, jnp.bfloat16)
    zero_memory = jnp.zeros(half_shape, jnp.float32)
    weight = None
    weight = lax.all_gather(gate_weight[0], "row", axis=0, tiled=True)
    moment_count = 4 + 2 * group_count
    for moment in range(moment_count):
        relative = moment - start_moment
        active = (relative >= 0) & (relative < 2 * group_count)
        group_index = jnp.clip(relative // 2, 0, group_count - 1)
        frame_index = jnp.clip(relative - 2 * group_index, 0, 1)
        is_first = frame_index == 0
        offset = group_index * group_rows
        mine_hidden = own_hidden
        mine_memory = own_memory
        fresh_input = lax.dynamic_slice(
            features,
            (offset, frame_index, 0, 0, 0),
            (group_rows, 1, tile_rows, tile_cols, channels),
        )[:, 0]
        from_before = jnp.where(
            (section_index == 2) & jnp.logical_not(is_first), context, recv_hidden
        )
        layer_input = jnp.where(section_index == 0, fresh_input, from_before)
        context = jnp.where((section_index == 2) & is_first, recv_hidden, context)
        kept_hidden = held_hidden
        kept_memory = held_memory
        start_hidden = jnp.where(
            section_index <= 1, zero_hidden, jnp.where(section_index == 2, recv_hidden, kept_hidden)
        )
        start_memory = jnp.where(
            section_index <= 1, zero_memory, jnp.where(section_index == 2, recv_memory, kept_memory)
        )
        prior_hidden = jnp.where(is_first, start_hidden, mine_hidden)
        prior_memory = jnp.where(is_first, start_memory, mine_memory)
        joined = jnp.concatenate([layer_input, prior_hidden], axis=-1)
        padded = with_halo(joined, (("row", 1), ("col", 2)), 1)
        layer_weight = weight

        def run_step(operands):
            padded_now, memory_now, unused_hidden, unused_memory = operands
            patches_now = make_patches(padded_now, tile_rows, tile_cols)
            gates_now = (
                jnp.dot(patches_now, layer_weight, preferred_element_type=jnp.float32) + layer_bias
            )
            hidden_new, memory_new = cell_update(
                gates_now, memory_now.reshape(-1, channels), channels
            )
            return (hidden_new.reshape(half_shape), memory_new.reshape(half_shape))

        def keep_step(operands):
            return (operands[2], operands[3])

        next_hidden, next_memory = lax.cond(
            active, run_step, keep_step, (padded, prior_memory, mine_hidden, mine_memory)
        )
        own_hidden = jnp.where(active, next_hidden, mine_hidden)
        own_memory = lax.dynamic_update_slice_in_dim(
            own_memory, jnp.where(active, next_memory, mine_memory), offset, 0
        )
        old_slot = lax.dynamic_slice(
            recorded,
            (offset, frame_index, 0, 0, 0),
            (group_rows, 1, tile_rows, tile_cols, channels),
        )
        recorded = lax.dynamic_update_slice(
            recorded,
            jnp.where(active, next_hidden[:, None], old_slot),
            (offset, frame_index, 0, 0, 0),
        )
        if moment < moment_count - 1:
            moved_hidden, recv_memory = (
                from_behind(
                    next_hidden.astype(jnp.float32).astype(jnp.bfloat16), "section", 1
                ).astype(jnp.float32),
                from_behind(shortened(next_memory), "section", 1).astype(next_memory.dtype),
            )
            recv_hidden = moved_hidden.astype(jnp.bfloat16)
        if moment % 2 == 1 and moment < 2 * group_count:
            got_hidden, got_memory = (
                from_behind(
                    next_hidden.astype(jnp.float32).astype(jnp.bfloat16), "section", 3
                ).astype(jnp.float32),
                from_behind(shortened(next_memory), "section", 3).astype(next_memory.dtype),
            )
            slot_start = moment // 2 * group_rows
            held_hidden = got_hidden.astype(jnp.bfloat16)
            held_memory = lax.dynamic_update_slice_in_dim(held_memory, got_memory, slot_start, 0)
    return recorded[None]


def solution(mesh):
    return jax.shard_map(
        local,
        mesh=mesh,
        in_specs=(P(None, None, "row", "col", None), P("section", "row", None), P("section", None)),
        out_specs=P("section", None, None, "row", "col", None),
        check_vma=False,
    )
```

profile of v0, /device:TPU:30, one launch (start us, length us, event | category | flops | bytes accessed | tf_op | source)
XLA Modules:
  0.0 171.6 jit_solution(16808412248618617733)
XLA Ops:
  8.2 1.3 collective-permute-start.1
  9.5 3.0 %collective-permute-start = (bf16[2,1,16,384]{3,2,1,0:T(8,128)(2,1)S(1)}, bf16[2,1,16,384]{3,2,1,0:T(8,128)(2,1)S(1)}, u32[]{:S(2)}, u32[]{:S(2)}) collective-permute-start(bf16[2,1,16,384]{3,2,1,0:T(8,128)(2,1)S(1)} %get-tuple-element.392), channel_id=1, source_target_pairs={{0,4},{1,5},{2,6},{3,7},{8,12},{9,13},{10,14},{11,15},{16,20},{17,... | collective-permute-start | bytes 73736 | tf_op jit(solution)/shard_map/ppermute | solution.py:14
  13.4 2.4 %collective-permute-start.3 = (bf16[2,6,1,384]{3,2,1,0:T(2,128)(2,1)S(1)}, bf16[2,6,1,384]{3,2,1,0:T(2,128)(2,1)S(1)}, u32[]{:S(2)}, u32[]{:S(2)}) collective-permute-start(bf16[2,6,1,384]{3,2,1,0:T(2,128)(2,1)S(1)} %get-tuple-element.367), channel_id=1, source_target_pairs={{1,0},{2,1},{3,2},{5,4},{6,5},{7,6},{9,8},{10,9},{11,10},{13,12},{... | collective-permute-start | bytes 27656 | tf_op jit(solution)/shard_map/ppermute | solution.py:15
  15.8 1.3 collective-permute-start.2
  17.2 4.2 %collective-permute-done.2 = bf16[2,6,1,384]{3,2,1,0:T(2,128)(2,1)S(1)} collective-permute-done((bf16[2,6,1,384]{3,2,1,0:T(2,128)(2,1)S(1)}, bf16[2,6,1,384]{3,2,1,0:T(2,128)(2,1)S(1)}, u32[]{:S(2)}, u32[]{:S(2)}) %collective-permute-start.2) | collective-permute-done | bytes 9248 | tf_op jit(solution)/shard_map/ppermute | solution.py:14
  21.5 3.9 %all-gather.3.cloned.1.call-done = bf16[1,3456,768]{2,1,0:T(8,128)(2,1)} async-done(((bf16[1,1728,768]{2,1,0:T(8,128)(2,1)}), bf16[1,3456,768]{2,1,0:T(8,128)(2,1)}) %all-gather.3.cloned.1.call-update) | async-done | bytes 5308432 | tf_op jit(solution)/shard_map/all_gather | solution.py:75
  25.5 1.3 collective-permute-start.4
  26.9 4.7 %collective-permute-done.4 = bf16[2,4,16,192]{3,2,1,0:T(8,128)(2,1)S(1)} collective-permute-done((bf16[2,4,16,192]{3,2,1,0:T(8,128)(2,1)S(1)}, bf16[2,4,16,192]{3,2,1,0:T(8,128)(2,1)S(1)}, u32[]{:S(2)}, u32[]{:S(2)}) %collective-permute-start.4) | collective-permute-done | bytes 49184 | tf_op jit(solution)/shard_map/ppermute | solution.py:31
  33.0 3.0 %collective-permute-start.5 = (bf16[2,1,16,384]{3,2,1,0:T(8,128)(2,1)S(1)}, bf16[2,1,16,384]{3,2,1,0:T(8,128)(2,1)S(1)}, u32[]{:S(2)}, u32[]{:S(2)}) collective-permute-start(bf16[2,1,16,384]{3,2,1,0:T(8,128)(2,1)S(1)} %get-tuple-element.384), channel_id=1, source_target_pairs={{0,4},{1,5},{2,6},{3,7},{8,12},{9,13},{10,14},{11,15},{16,20},{17,... | collective-permute-start | bytes 73736 | tf_op jit(solution)/shard_map/ppermute | solution.py:14
  36.1 1.3 collective-permute-start.9
  37.6 2.4 %collective-permute-start.8 = (bf16[2,6,1,384]{3,2,1,0:T(2,128)(2,1)S(1)}, bf16[2,6,1,384]{3,2,1,0:T(2,128)(2,1)S(1)}, u32[]{:S(2)}, u32[]{:S(2)}) collective-permute-start(bf16[2,6,1,384]{3,2,1,0:T(2,128)(2,1)S(1)} %get-tuple-element.365), channel_id=1, source_target_pairs={{1,0},{2,1},{3,2},{5,4},{6,5},{7,6},{9,8},{10,9},{11,10},{13,12},{... | collective-permute-start | bytes 27656 | tf_op jit(solution)/shard_map/ppermute | solution.py:15
  40.0 1.3 collective-permute-start.7
  42.3 3.4 %collective-permute-done.7 = bf16[2,6,1,384]{3,2,1,0:T(2,128)(2,1)S(1)} collective-permute-done((bf16[2,6,1,384]{3,2,1,0:T(2,128)(2,1)S(1)}, bf16[2,6,1,384]{3,2,1,0:T(2,128)(2,1)S(1)}, u32[]{:S(2)}, u32[]{:S(2)}) %collective-permute-start.7) | collective-permute-done | bytes 9248 | tf_op jit(solution)/shard_map/ppermute | solution.py:14
  46.5 1.3 collective-permute-start.10
  47.8 1.3 collective-permute-start.11
  49.1 4.4 %collective-permute-done.10 = bf16[2,4,16,192]{3,2,1,0:T(8,128)(2,1)S(1)} collective-permute-done((bf16[2,4,16,192]{3,2,1,0:T(8,128)(2,1)}, bf16[2,4,16,192]{3,2,1,0:T(8,128)(2,1)S(1)}, u32[]{:S(2)}, u32[]{:S(2)}) %collective-permute-start.10) | collective-permute-done | bytes 49184 | tf_op jit(solution)/shard_map/ppermute | solution.py:31
  53.5 9.6 %collective-permute-done.11 = bf16[2,4,16,192]{3,2,1,0:T(8,128)(2,1)S(1)} collective-permute-done((bf16[2,4,16,192]{3,2,1,0:T(8,128)(2,1)}, bf16[2,4,16,192]{3,2,1,0:T(8,128)(2,1)S(1)}, u32[]{:S(2)}, u32[]{:S(2)}) %collective-permute-start.11) | collective-permute-done | bytes 49184 | tf_op jit(solution)/shard_map/ppermute | solution.py:31
  64.4 3.0 %collective-permute-start.12 = (bf16[2,1,16,384]{3,2,1,0:T(8,128)(2,1)S(1)}, bf16[2,1,16,384]{3,2,1,0:T(8,128)(2,1)S(1)}, u32[]{:S(2)}, u32[]{:S(2)}) collective-permute-start(bf16[2,1,16,384]{3,2,1,0:T(8,128)(2,1)S(1)} %get-tuple-element.380), channel_id=1, source_target_pairs={{0,4},{1,5},{2,6},{3,7},{8,12},{9,13},{10,14},{11,15},{16,20},{17,... | collective-permute-start | bytes 73736 | tf_op jit(solution)/shard_map/ppermute | solution.py:14
  67.5 1.3 collective-permute-start.16
  68.8 1.3 collective-permute-start.17
  70.3 2.4 %collective-permute-start.15 = (bf16[2,6,1,384]{3,2,1,0:T(2,128)(2,1)S(1)}, bf16[2,6,1,384]{3,2,1,0:T(2,128)(2,1)S(1)}, u32[]{:S(2)}, u32[]{:S(2)}) collective-permute-start(bf16[2,6,1,384]{3,2,1,0:T(2,128)(2,1)S(1)} %get-tuple-element.363), channel_id=1, source_target_pairs={{1,0},{2,1},{3,2},{5,4},{6,5},{7,6},{9,8},{10,9},{11,10},{13,12},{... | collective-permute-start | bytes 27656 | tf_op jit(solution)/shard_map/ppermute | solution.py:15
  72.7 1.3 collective-permute-start.14
  74.1 1.7 %collective-permute-done.17 = bf16[2,4,16,192]{3,2,1,0:T(8,128)(2,1)S(1)} collective-permute-done((bf16[2,4,16,192]{3,2,1,0:T(8,128)(2,1)S(1)}, bf16[2,4,16,192]{3,2,1,0:T(8,128)(2,1)S(1)}, u32[]{:S(2)}, u32[]{:S(2)}) %collective-permute-start.17) | collective-permute-done | bytes 49184 | tf_op jit(solution)/shard_map/ppermute | solution.py:31
  75.9 2.5 %collective-permute-done.14 = bf16[2,6,1,384]{3,2,1,0:T(2,128)(2,1)S(1)} collective-permute-done((bf16[2,6,1,384]{3,2,1,0:T(2,128)(2,1)S(1)}, bf16[2,6,1,384]{3,2,1,0:T(2,128)(2,1)S(1)}, u32[]{:S(2)}, u32[]{:S(2)}) %collective-permute-start.14) | collective-permute-done | bytes 9248 | tf_op jit(solution)/shard_map/ppermute | solution.py:14
  79.2 1.3 collective-permute-start.18
  80.5 5.0 %collective-permute-done.18 = bf16[2,4,16,192]{3,2,1,0:T(8,128)(2,1)S(1)} collective-permute-done((bf16[2,4,16,192]{3,2,1,0:T(8,128)(2,1)}, bf16[2,4,16,192]{3,2,1,0:T(8,128)(2,1)S(1)}, u32[]{:S(2)}, u32[]{:S(2)}) %collective-permute-start.18) | collective-permute-done | bytes 49184 | tf_op jit(solution)/shard_map/ppermute | solution.py:31
  87.0 3.0 %collective-permute-start.19 = (bf16[2,1,16,384]{3,2,1,0:T(8,128)(2,1)S(1)}, bf16[2,1,16,384]{3,2,1,0:T(8,128)(2,1)S(1)}, u32[]{:S(2)}, u32[]{:S(2)}) collective-permute-start(bf16[2,1,16,384]{3,2,1,0:T(8,128)(2,1)S(1)} %get-tuple-element.376), channel_id=1, source_target_pairs={{0,4},{1,5},{2,6},{3,7},{8,12},{9,13},{10,14},{11,15},{16,20},{17,... | collective-permute-start | bytes 73736 | tf_op jit(solution)/shard_map/ppermute | solution.py:14
  90.0 1.3 collective-permute-start.23
  91.5 2.1 %collective-permute-start.22 = (bf16[2,6,1,384]{3,2,1,0:T(2,128)(2,1)S(1)}, bf16[2,6,1,384]{3,2,1,0:T(2,128)(2,1)S(1)}, u32[]{:S(2)}, u32[]{:S(2)}) collective-permute-start(bf16[2,6,1,384]{3,2,1,0:T(2,128)(2,1)S(1)} %get-tuple-element.361), channel_id=1, source_target_pairs={{1,0},{2,1},{3,2},{5,4},{6,5},{7,6},{9,8},{10,9},{11,10},{13,12},{... | collective-permute-start | bytes 27656 | tf_op jit(solution)/shard_map/ppermute | solution.py:15
  93.6 1.3 collective-permute-start.21
  95.0 4.3 %collective-permute-done.23 = bf16[2,4,16,192]{3,2,1,0:T(8,128)(2,1)S(1)} collective-permute-done((bf16[2,4,16,192]{3,2,1,0:T(8,128)(2,1)S(1)}, bf16[2,4,16,192]{3,2,1,0:T(8,128)(2,1)S(1)}, u32[]{:S(2)}, u32[]{:S(2)}) %collective-permute-start.23) | collective-permute-done | bytes 49184 | tf_op jit(solution)/shard_map/ppermute | solution.py:31
  100.1 1.3 collective-permute-start.24
  101.5 14.2 %collective-permute-done.24 = bf16[2,4,16,192]{3,2,1,0:T(8,128)(2,1)S(1)} collective-permute-done((bf16[2,4,16,192]{3,2,1,0:T(8,128)(2,1)}, bf16[2,4,16,192]{3,2,1,0:T(8,128)(2,1)S(1)}, u32[]{:S(2)}, u32[]{:S(2)}) %collective-permute-start.24) | collective-permute-done | bytes 49184 | tf_op jit(solution)/shard_map/ppermute | solution.py:31
  117.1 3.0 %collective-permute-start.25 = (bf16[2,1,16,384]{3,2,1,0:T(8,128)(2,1)S(1)}, bf16[2,1,16,384]{3,2,1,0:T(8,128)(2,1)S(1)}, u32[]{:S(2)}, u32[]{:S(2)}) collective-permute-start(bf16[2,1,16,384]{3,2,1,0:T(8,128)(2,1)S(1)} %get-tuple-element.372), channel_id=1, source_target_pairs={{0,4},{1,5},{2,6},{3,7},{8,12},{9,13},{10,14},{11,15},{16,20},{17,... | collective-permute-start | bytes 73736 | tf_op jit(solution)/shard_map/ppermute | solution.py:14
  120.1 1.3 collective-permute-start.29
  121.6 1.9 %collective-permute-start.28 = (bf16[2,6,1,384]{3,2,1,0:T(2,128)(2,1)S(1)}, bf16[2,6,1,384]{3,2,1,0:T(2,128)(2,1)S(1)}, u32[]{:S(2)}, u32[]{:S(2)}) collective-permute-start(bf16[2,6,1,384]{3,2,1,0:T(2,128)(2,1)S(1)} %get-tuple-element.359), channel_id=1, source_target_pairs={{1,0},{2,1},{3,2},{5,4},{6,5},{7,6},{9,8},{10,9},{11,10},{13,12},{... | collective-permute-start | bytes 27656 | tf_op jit(solution)/shard_map/ppermute | solution.py:15
  124.9 3.1 %collective-permute-done.29 = bf16[2,4,16,192]{3,2,1,0:T(8,128)(2,1)S(1)} collective-permute-done((bf16[2,4,16,192]{3,2,1,0:T(8,128)(2,1)S(1)}, bf16[2,4,16,192]{3,2,1,0:T(8,128)(2,1)S(1)}, u32[]{:S(2)}, u32[]{:S(2)}) %collective-permute-start.29) | collective-permute-done | bytes 49184 | tf_op jit(solution)/shard_map/ppermute | solution.py:31
  129.3 6.2 %conditional.10 = (bf16[2,4,16,192]{3,2,1,0:T(8,128)(2,1)}, f32[2,4,16,192]{3,2,1,0:T(8,128)S(1)}, bf16[2,1,4,16,192]{4,3,2,0,1:T(8,128)(2,1)S(1)}) conditional(s32[]{:T(128)} %convert_element_type.114, (bf16[2,4,16,192]{3,2,1,0:T(8,128)(2,1)S(1)}, f32[2,4,16,192]{3,2,1,0:T(8,128)S(1)}) %tuple.76, (bf16[2,6,18,384]{3,2,1,0:T(8,128)(2,1)S(1)}, ...), branch_computations={%region_8.9_spmd, %region_9.10_spmd} | conditional | flops 679993344 | bytes 9593887 | solution.py:124
  130.3 3.5 %convolution_add_fusion.4 = f32[128,768]{1,0:T(8,128)S(1)} fusion(bf16[128,3456]{1,0:T(8,128)(2,1)S(1)} %bitcast.90, bf16[3456,768]{1,0:T(8,128)(2,1)} %get-tuple-element.283, f32[768]{0:T(1024)S(1)} %reduce.4), kind=kOutput, calls=%fused_computation.116 | convolution fusion | flops 679575552 | bytes 6589440 | tf_op jit(solution)/shard_map/cond/branch_1_fun/dot_general | solution.py:114
  136.8 7.4 %collective-permute-done.30 = bf16[2,4,16,192]{3,2,1,0:T(8,128)(2,1)S(1)} collective-permute-done((bf16[2,4,16,192]{3,2,1,0:T(8,128)(2,1)}, bf16[2,4,16,192]{3,2,1,0:T(8,128)(2,1)S(1)}, u32[]{:S(2)}, u32[]{:S(2)}) %collective-permute-start.30) | collective-permute-done | bytes 49184 | tf_op jit(solution)/shard_map/ppermute | solution.py:31
  146.4 3.0 %collective-permute-start.31 = (bf16[2,1,16,384]{3,2,1,0:T(8,128)(2,1)S(1)}, bf16[2,1,16,384]{3,2,1,0:T(8,128)(2,1)S(1)}, u32[]{:S(2)}, u32[]{:S(2)}) collective-permute-start(bf16[2,1,16,384]{3,2,1,0:T(8,128)(2,1)S(1)} %get-tuple-element.368), channel_id=1, source_target_pairs={{0,4},{1,5},{2,6},{3,7},{8,12},{9,13},{10,14},{11,15},{16,20},{17,... | collective-permute-start | bytes 73736 | tf_op jit(solution)/shard_map/ppermute | solution.py:14
  150.2 1.3 collective-permute-start.35
  151.7 1.9 %collective-permute-start.34 = (bf16[2,6,1,384]{3,2,1,0:T(2,128)(2,1)S(1)}, bf16[2,6,1,384]{3,2,1,0:T(2,128)(2,1)S(1)}, u32[]{:S(2)}, u32[]{:S(2)}) collective-permute-start(bf16[2,6,1,384]{3,2,1,0:T(2,128)(2,1)S(1)} %get-tuple-element.357), channel_id=1, source_target_pairs={{1,0},{2,1},{3,2},{5,4},{6,5},{7,6},{9,8},{10,9},{11,10},{13,12},{... | collective-permute-start | bytes 27656 | tf_op jit(solution)/shard_map/ppermute | solution.py:15
  153.6 1.3 collective-permute-start.33
  155.0 2.3 %collective-permute-done.35 = bf16[2,4,16,192]{3,2,1,0:T(8,128)(2,1)S(1)} collective-permute-done((bf16[2,4,16,192]{3,2,1,0:T(8,128)(2,1)S(1)}, bf16[2,4,16,192]{3,2,1,0:T(8,128)(2,1)S(1)}, u32[]{:S(2)}, u32[]{:S(2)}) %collective-permute-start.35) | collective-permute-done | bytes 49184 | tf_op jit(solution)/shard_map/ppermute | solution.py:31
  157.3 2.0 %collective-permute-done.33 = bf16[2,6,1,384]{3,2,1,0:T(2,128)(2,1)S(1)} collective-permute-done((bf16[2,6,1,384]{3,2,1,0:T(2,128)(2,1)S(1)}, bf16[2,6,1,384]{3,2,1,0:T(2,128)(2,1)S(1)}, u32[]{:S(2)}, u32[]{:S(2)}) %collective-permute-start.33) | collective-permute-done | bytes 9248 | tf_op jit(solution)/shard_map/ppermute | solution.py:14
  159.4 4.7 %conditional.11 = (bf16[2,1,4,16,192]{4,3,2,0,1:T(8,128)(2,1)S(1)}) conditional(s32[]{:T(128)} %convert_element_type.117, bf16[2,4,16,192]{3,2,1,0:T(8,128)(2,1)S(1)} %get-tuple-element.345, (bf16[2,6,18,384]{3,2,1,0:T(8,128)(2,1)S(1)}, bf16[2,6,16,384]{3,2,1,0:T(8,128)(2,1)S(1)}, bf16[2,4,16,384]{3,2,1,0:T(8,128)(2,1)S(1)}, ...), branch_computations={%region_10.11_spmd, %region_11.12_spmd} | conditional | flops 680017920 | bytes 9544718 | solution.py:124
  160.4 3.5 %convolution_add_fusion.5 = f32[128,768]{1,0:T(8,128)S(1)} fusion(bf16[128,3456]{1,0:T(8,128)(2,1)S(1)} %bitcast.91, bf16[3456,768]{1,0:T(8,128)(2,1)} %get-tuple-element.295, f32[768]{0:T(1024)S(1)} %reduce.5), kind=kOutput, calls=%fused_computation.145 | convolution fusion | flops 679575552 | bytes 6589440 | tf_op jit(solution)/shard_map/cond/branch_1_fun/dot_general | solution.py:114
  (131 shorter events, 26.3 us)
Async XLA Ops:
  6.5 18.9 %all-gather.3.cloned.1.call-start = ((), (), s32[]{:S(2)}) async-start(), calls=%async_computation | async-start | bytes 7962624 | tf_op jit(solution)/shard_map/all_gather | solution.py:75
  8.2 4.4 %collective-permute-start.1 = (bf16[2,1,16,384]{3,2,1,0:T(8,128)(2,1)S(1)}, bf16[2,1,16,384]{3,2,1,0:T(8,128)(2,1)S(1)}, u32[]{:S(2)}, u32[]{:S(2)}) collective-permute-start(bf16[2,1,16,384]{3,2,1,0:T(8,128)(2,1)S(1)} %get-tuple-element.393), channel_id=1, source_target_pairs={{4,0},{5,1},{6,2},{7,3},{12,8},{13,9},{14,10},{15,11},{20,16},{21,... | collective-permute-start | bytes 73736 | tf_op jit(solution)/shard_map/ppermute | solution.py:15
  9.5 3.9 %collective-permute-start = (bf16[2,1,16,384]{3,2,1,0:T(8,128)(2,1)S(1)}, bf16[2,1,16,384]{3,2,1,0:T(8,128)(2,1)S(1)}, u32[]{:S(2)}, u32[]{:S(2)}) collective-permute-start(bf16[2,1,16,384]{3,2,1,0:T(8,128)(2,1)S(1)} %get-tuple-element.392), channel_id=1, source_target_pairs={{0,4},{1,5},{2,6},{3,7},{8,12},{9,13},{10,14},{11,15},{16,20},{17,... | collective-permute-start | bytes 73736 | tf_op jit(solution)/shard_map/ppermute | solution.py:14
  12.5 19.1 %copy-start = (bf16[2,2,4,16,192]{4,3,2,1,0:T(8,128)(2,1)S(1)}, bf16[2,2,4,16,192]{4,3,2,1,0:T(8,128)(2,1)}, u32[]{:S(2)}) copy-start(bf16[2,2,4,16,192]{4,3,2,1,0:T(8,128)(2,1)} %param.15) | copy-start | bytes 294916
  13.4 3.8 %collective-permute-start.3 = (bf16[2,6,1,384]{3,2,1,0:T(2,128)(2,1)S(1)}, bf16[2,6,1,384]{3,2,1,0:T(2,128)(2,1)S(1)}, u32[]{:S(2)}, u32[]{:S(2)}) collective-permute-start(bf16[2,6,1,384]{3,2,1,0:T(2,128)(2,1)S(1)} %get-tuple-element.367), channel_id=1, source_target_pairs={{1,0},{2,1},{3,2},{5,4},{6,5},{7,6},{9,8},{10,9},{11,10},{13,12},{... | collective-permute-start | bytes 27656 | tf_op jit(solution)/shard_map/ppermute | solution.py:15
  15.8 5.7 %collective-permute-start.2 = (bf16[2,6,1,384]{3,2,1,0:T(2,128)(2,1)S(1)}, bf16[2,6,1,384]{3,2,1,0:T(2,128)(2,1)S(1)}, u32[]{:S(2)}, u32[]{:S(2)}) collective-permute-start(bf16[2,6,1,384]{3,2,1,0:T(2,128)(2,1)S(1)} %get-tuple-element.366), channel_id=1, source_target_pairs={{0,1},{1,2},{2,3},{4,5},{5,6},{6,7},{8,9},{9,10},{10,11},{12,13},{... | collective-permute-start | bytes 27656 | tf_op jit(solution)/shard_map/ppermute | solution.py:14
  25.5 6.2 %collective-permute-start.4 = (bf16[2,4,16,192]{3,2,1,0:T(8,128)(2,1)S(1)}, bf16[2,4,16,192]{3,2,1,0:T(8,128)(2,1)S(1)}, u32[]{:S(2)}, u32[]{:S(2)}) collective-permute-start(bf16[2,4,16,192]{3,2,1,0:T(8,128)(2,1)S(1)} %get-tuple-element.320), channel_id=1, source_target_pairs={{0,8},{8,16},{16,24},{1,9},{9,17},{17,25},{2,10},{10,18},{18,26},{... | collective-permute-start | bytes 147464 | tf_op jit(solution)/shard_map/ppermute | solution.py:31
  31.7 5.7 %collective-permute-start.6 = (bf16[2,1,16,384]{3,2,1,0:T(8,128)(2,1)S(1)}, bf16[2,1,16,384]{3,2,1,0:T(8,128)(2,1)S(1)}, u32[]{:S(2)}, u32[]{:S(2)}) collective-permute-start(bf16[2,1,16,384]{3,2,1,0:T(8,128)(2,1)S(1)} %get-tuple-element.385), channel_id=1, source_target_pairs={{4,0},{5,1},{6,2},{7,3},{12,8},{13,9},{14,10},{15,11},{20,16},{21,... | collective-permute-start | bytes 73736 | tf_op jit(solution)/shard_map/ppermute | solution.py:15
  33.0 4.4 %collective-permute-start.5 = (bf16[2,1,16,384]{3,2,1,0:T(8,128)(2,1)S(1)}, bf16[2,1,16,384]{3,2,1,0:T(8,128)(2,1)S(1)}, u32[]{:S(2)}, u32[]{:S(2)}) collective-permute-start(bf16[2,1,16,384]{3,2,1,0:T(8,128)(2,1)S(1)} %get-tuple-element.384), channel_id=1, source_target_pairs={{0,4},{1,5},{2,6},{3,7},{8,12},{9,13},{10,14},{11,15},{16,20},{17,... | collective-permute-start | bytes 73736 | tf_op jit(solution)/shard_map/ppermute | solution.py:14
  36.1 6.2 %collective-permute-start.9 = (bf16[2,4,16,192]{3,2,1,0:T(8,128)(2,1)S(1)}, bf16[2,4,16,192]{3,2,1,0:T(8,128)(2,1)S(1)}, u32[]{:S(2)}, u32[]{:S(2)}) collective-permute-start(bf16[2,4,16,192]{3,2,1,0:T(8,128)(2,1)S(1)} %get-tuple-element.382), channel_id=1, source_target_pairs={{0,8},{8,16},{16,24},{1,9},{9,17},{17,25},{2,10},{10,18},{18,26},{... | collective-permute-start | bytes 147464 | tf_op jit(solution)/shard_map/ppermute | solution.py:31
  37.6 4.7 %collective-permute-start.8 = (bf16[2,6,1,384]{3,2,1,0:T(2,128)(2,1)S(1)}, bf16[2,6,1,384]{3,2,1,0:T(2,128)(2,1)S(1)}, u32[]{:S(2)}, u32[]{:S(2)}) collective-permute-start(bf16[2,6,1,384]{3,2,1,0:T(2,128)(2,1)S(1)} %get-tuple-element.365), channel_id=1, source_target_pairs={{1,0},{2,1},{3,2},{5,4},{6,5},{7,6},{9,8},{10,9},{11,10},{13,12},{... | collective-permute-start | bytes 27656 | tf_op jit(solution)/shard_map/ppermute | solution.py:15
  40.0 5.7 %collective-permute-start.7 = (bf16[2,6,1,384]{3,2,1,0:T(2,128)(2,1)S(1)}, bf16[2,6,1,384]{3,2,1,0:T(2,128)(2,1)S(1)}, u32[]{:S(2)}, u32[]{:S(2)}) collective-permute-start(bf16[2,6,1,384]{3,2,1,0:T(2,128)(2,1)S(1)} %get-tuple-element.364), channel_id=1, source_target_pairs={{0,1},{1,2},{2,3},{4,5},{5,6},{6,7},{8,9},{9,10},{10,11},{12,13},{... | collective-permute-start | bytes 27656 | tf_op jit(solution)/shard_map/ppermute | solution.py:14
  46.5 7.0 %collective-permute-start.10 = (bf16[2,4,16,192]{3,2,1,0:T(8,128)(2,1)}, bf16[2,4,16,192]{3,2,1,0:T(8,128)(2,1)S(1)}, u32[]{:S(2)}, u32[]{:S(2)}) collective-permute-start(bf16[2,4,16,192]{3,2,1,0:T(8,128)(2,1)} %get-tuple-element.323), channel_id=1, source_target_pairs={{0,8},{8,16},{16,24},{1,9},{9,17},{17,25},{2,10},{10,18},{18,26},{... | collective-permute-start | bytes 147464 | tf_op jit(solution)/shard_map/ppermute | solution.py:31
  47.8 15.3 %collective-permute-start.11 = (bf16[2,4,16,192]{3,2,1,0:T(8,128)(2,1)}, bf16[2,4,16,192]{3,2,1,0:T(8,128)(2,1)S(1)}, u32[]{:S(2)}, u32[]{:S(2)}) collective-permute-start(bf16[2,4,16,192]{3,2,1,0:T(8,128)(2,1)} %get-tuple-element.323), channel_id=1, source_target_pairs={{0,24},{1,25},{2,26},{3,27},{4,28},{5,29},{6,30},{7,31}} | collective-permute-start | bytes 147464 | tf_op jit(solution)/shard_map/ppermute | solution.py:31
  63.2 7.0 %collective-permute-start.13 = (bf16[2,1,16,384]{3,2,1,0:T(8,128)(2,1)S(1)}, bf16[2,1,16,384]{3,2,1,0:T(8,128)(2,1)S(1)}, u32[]{:S(2)}, u32[]{:S(2)}) collective-permute-start(bf16[2,1,16,384]{3,2,1,0:T(8,128)(2,1)S(1)} %get-tuple-element.381), channel_id=1, source_target_pairs={{4,0},{5,1},{6,2},{7,3},{12,8},{13,9},{14,10},{15,11},{20,16},{21,... | collective-permute-start | bytes 73736 | tf_op jit(solution)/shard_map/ppermute | solution.py:15
  64.4 5.7 %collective-permute-start.12 = (bf16[2,1,16,384]{3,2,1,0:T(8,128)(2,1)S(1)}, bf16[2,1,16,384]{3,2,1,0:T(8,128)(2,1)S(1)}, u32[]{:S(2)}, u32[]{:S(2)}) collective-permute-start(bf16[2,1,16,384]{3,2,1,0:T(8,128)(2,1)S(1)} %get-tuple-element.380), channel_id=1, source_target_pairs={{0,4},{1,5},{2,6},{3,7},{8,12},{9,13},{10,14},{11,15},{16,20},{17,... | collective-permute-start | bytes 73736 | tf_op jit(solution)/shard_map/ppermute | solution.py:14
  67.5 6.6 %collective-permute-start.16 = (bf16[2,4,16,192]{3,2,1,0:T(8,128)(2,1)S(1)}, bf16[2,4,16,192]{3,2,1,0:T(8,128)(2,1)S(1)}, u32[]{:S(2)}, u32[]{:S(2)}) collective-permute-start(bf16[2,4,16,192]{3,2,1,0:T(8,128)(2,1)S(1)} %get-tuple-element.378), channel_id=1, source_target_pairs={{0,8},{8,16},{16,24},{1,9},{9,17},{17,25},{2,10},{10,18},{18,26},{... | collective-permute-start | bytes 147464 | tf_op jit(solution)/shard_map/ppermute | solution.py:31
  68.8 7.1 %collective-permute-start.17 = (bf16[2,4,16,192]{3,2,1,0:T(8,128)(2,1)S(1)}, bf16[2,4,16,192]{3,2,1,0:T(8,128)(2,1)S(1)}, u32[]{:S(2)}, u32[]{:S(2)}) collective-permute-start(bf16[2,4,16,192]{3,2,1,0:T(8,128)(2,1)S(1)} %get-tuple-element.378), channel_id=1, source_target_pairs={{0,24},{1,25},{2,26},{3,27},{4,28},{5,29},{6,30},{7,31}} | collective-permute-start | bytes 147464 | tf_op jit(solution)/shard_map/ppermute | solution.py:31
  70.3 5.6 %collective-permute-start.15 = (bf16[2,6,1,384]{3,2,1,0:T(2,128)(2,1)S(1)}, bf16[2,6,1,384]{3,2,1,0:T(2,128)(2,1)S(1)}, u32[]{:S(2)}, u32[]{:S(2)}) collective-permute-start(bf16[2,6,1,384]{3,2,1,0:T(2,128)(2,1)S(1)} %get-tuple-element.363), channel_id=1, source_target_pairs={{1,0},{2,1},{3,2},{5,4},{6,5},{7,6},{9,8},{10,9},{11,10},{13,12},{... | collective-permute-start | bytes 27656 | tf_op jit(solution)/shard_map/ppermute | solution.py:15
  72.7 5.7 %collective-permute-start.14 = (bf16[2,6,1,384]{3,2,1,0:T(2,128)(2,1)S(1)}, bf16[2,6,1,384]{3,2,1,0:T(2,128)(2,1)S(1)}, u32[]{:S(2)}, u32[]{:S(2)}) collective-permute-start(bf16[2,6,1,384]{3,2,1,0:T(2,128)(2,1)S(1)} %get-tuple-element.362), channel_id=1, source_target_pairs={{0,1},{1,2},{2,3},{4,5},{5,6},{6,7},{8,9},{9,10},{10,11},{12,13},{... | collective-permute-start | bytes 27656 | tf_op jit(solution)/shard_map/ppermute | solution.py:14
  79.2 6.4 %collective-permute-start.18 = (bf16[2,4,16,192]{3,2,1,0:T(8,128)(2,1)}, bf16[2,4,16,192]{3,2,1,0:T(8,128)(2,1)S(1)}, u32[]{:S(2)}, u32[]{:S(2)}) collective-permute-start(bf16[2,4,16,192]{3,2,1,0:T(8,128)(2,1)} %get-tuple-element.326), channel_id=1, source_target_pairs={{0,8},{8,16},{16,24},{1,9},{9,17},{17,25},{2,10},{10,18},{18,26},{... | collective-permute-start | bytes 147464 | tf_op jit(solution)/shard_map/ppermute | solution.py:31
  85.7 5.7 %collective-permute-start.20 = (bf16[2,1,16,384]{3,2,1,0:T(8,128)(2,1)S(1)}, bf16[2,1,16,384]{3,2,1,0:T(8,128)(2,1)S(1)}, u32[]{:S(2)}, u32[]{:S(2)}) collective-permute-start(bf16[2,1,16,384]{3,2,1,0:T(8,128)(2,1)S(1)} %get-tuple-element.377), channel_id=1, source_target_pairs={{4,0},{5,1},{6,2},{7,3},{12,8},{13,9},{14,10},{15,11},{20,16},{21,... | collective-permute-start | bytes 73736 | tf_op jit(solution)/shard_map/ppermute | solution.py:15
  87.0 4.4 %collective-permute-start.19 = (bf16[2,1,16,384]{3,2,1,0:T(8,128)(2,1)S(1)}, bf16[2,1,16,384]{3,2,1,0:T(8,128)(2,1)S(1)}, u32[]{:S(2)}, u32[]{:S(2)}) collective-permute-start(bf16[2,1,16,384]{3,2,1,0:T(8,128)(2,1)S(1)} %get-tuple-element.376), channel_id=1, source_target_pairs={{0,4},{1,5},{2,6},{3,7},{8,12},{9,13},{10,14},{11,15},{16,20},{17,... | collective-permute-start | bytes 73736 | tf_op jit(solution)/shard_map/ppermute | solution.py:14
  90.0 9.2 %collective-permute-start.23 = (bf16[2,4,16,192]{3,2,1,0:T(8,128)(2,1)S(1)}, bf16[2,4,16,192]{3,2,1,0:T(8,128)(2,1)S(1)}, u32[]{:S(2)}, u32[]{:S(2)}) collective-permute-start(bf16[2,4,16,192]{3,2,1,0:T(8,128)(2,1)S(1)} %get-tuple-element.374), channel_id=1, source_target_pairs={{0,8},{8,16},{16,24},{1,9},{9,17},{17,25},{2,10},{10,18},{18,26},{... | collective-permute-start | bytes 147464 | tf_op jit(solution)/shard_map/ppermute | solution.py:31
  91.5 7.8 %collective-permute-start.22 = (bf16[2,6,1,384]{3,2,1,0:T(2,128)(2,1)S(1)}, bf16[2,6,1,384]{3,2,1,0:T(2,128)(2,1)S(1)}, u32[]{:S(2)}, u32[]{:S(2)}) collective-permute-start(bf16[2,6,1,384]{3,2,1,0:T(2,128)(2,1)S(1)} %get-tuple-element.361), channel_id=1, source_target_pairs={{1,0},{2,1},{3,2},{5,4},{6,5},{7,6},{9,8},{10,9},{11,10},{13,12},{... | collective-permute-start | bytes 27656 | tf_op jit(solution)/shard_map/ppermute | solution.py:15
  93.6 5.7 %collective-permute-start.21 = (bf16[2,6,1,384]{3,2,1,0:T(2,128)(2,1)S(1)}, bf16[2,6,1,384]{3,2,1,0:T(2,128)(2,1)S(1)}, u32[]{:S(2)}, u32[]{:S(2)}) collective-permute-start(bf16[2,6,1,384]{3,2,1,0:T(2,128)(2,1)S(1)} %get-tuple-element.360), channel_id=1, source_target_pairs={{0,1},{1,2},{2,3},{4,5},{5,6},{6,7},{8,9},{9,10},{10,11},{12,13},{... | collective-permute-start | bytes 27656 | tf_op jit(solution)/shard_map/ppermute | solution.py:14
  100.1 15.5 %collective-permute-start.24 = (bf16[2,4,16,192]{3,2,1,0:T(8,128)(2,1)}, bf16[2,4,16,192]{3,2,1,0:T(8,128)(2,1)S(1)}, u32[]{:S(2)}, u32[]{:S(2)}) collective-permute-start(bf16[2,4,16,192]{3,2,1,0:T(8,128)(2,1)} %get-tuple-element.329), channel_id=1, source_target_pairs={{0,8},{8,16},{16,24},{1,9},{9,17},{17,25},{2,10},{10,18},{18,26},{... | collective-permute-start | bytes 147464 | tf_op jit(solution)/shard_map/ppermute | solution.py:31
  115.8 5.7 %collective-permute-start.26 = (bf16[2,1,16,384]{3,2,1,0:T(8,128)(2,1)S(1)}, bf16[2,1,16,384]{3,2,1,0:T(8,128)(2,1)S(1)}, u32[]{:S(2)}, u32[]{:S(2)}) collective-permute-start(bf16[2,1,16,384]{3,2,1,0:T(8,128)(2,1)S(1)} %get-tuple-element.373), channel_id=1, source_target_pairs={{4,0},{5,1},{6,2},{7,3},{12,8},{13,9},{14,10},{15,11},{20,16},{21,... | collective-permute-start | bytes 73736 | tf_op jit(solution)/shard_map/ppermute | solution.py:15
  117.1 4.4 %collective-permute-start.25 = (bf16[2,1,16,384]{3,2,1,0:T(8,128)(2,1)S(1)}, bf16[2,1,16,384]{3,2,1,0:T(8,128)(2,1)S(1)}, u32[]{:S(2)}, u32[]{:S(2)}) collective-permute-start(bf16[2,1,16,384]{3,2,1,0:T(8,128)(2,1)S(1)} %get-tuple-element.372), channel_id=1, source_target_pairs={{0,4},{1,5},{2,6},{3,7},{8,12},{9,13},{10,14},{11,15},{16,20},{17,... | collective-permute-start | bytes 73736 | tf_op jit(solution)/shard_map/ppermute | solution.py:14
  120.1 7.9 %collective-permute-start.29 = (bf16[2,4,16,192]{3,2,1,0:T(8,128)(2,1)S(1)}, bf16[2,4,16,192]{3,2,1,0:T(8,128)(2,1)S(1)}, u32[]{:S(2)}, u32[]{:S(2)}) collective-permute-start(bf16[2,4,16,192]{3,2,1,0:T(8,128)(2,1)S(1)} %get-tuple-element.370), channel_id=1, source_target_pairs={{0,8},{8,16},{16,24},{1,9},{9,17},{17,25},{2,10},{10,18},{18,26},{... | collective-permute-start | bytes 147464 | tf_op jit(solution)/shard_map/ppermute | solution.py:31
  121.6 6.5 %collective-permute-start.28 = (bf16[2,6,1,384]{3,2,1,0:T(2,128)(2,1)S(1)}, bf16[2,6,1,384]{3,2,1,0:T(2,128)(2,1)S(1)}, u32[]{:S(2)}, u32[]{:S(2)}) collective-permute-start(bf16[2,6,1,384]{3,2,1,0:T(2,128)(2,1)S(1)} %get-tuple-element.359), channel_id=1, source_target_pairs={{1,0},{2,1},{3,2},{5,4},{6,5},{7,6},{9,8},{10,9},{11,10},{13,12},{... | collective-permute-start | bytes 27656 | tf_op jit(solution)/shard_map/ppermute | solution.py:15
  123.5 5.7 %collective-permute-start.27 = (bf16[2,6,1,384]{3,2,1,0:T(2,128)(2,1)S(1)}, bf16[2,6,1,384]{3,2,1,0:T(2,128)(2,1)S(1)}, u32[]{:S(2)}, u32[]{:S(2)}) collective-permute-start(bf16[2,6,1,384]{3,2,1,0:T(2,128)(2,1)S(1)} %get-tuple-element.358), channel_id=1, source_target_pairs={{0,1},{1,2},{2,3},{4,5},{5,6},{6,7},{8,9},{9,10},{10,11},{12,13},{... | collective-permute-start | bytes 27656 | tf_op jit(solution)/shard_map/ppermute | solution.py:14
  135.5 8.7 %collective-permute-start.30 = (bf16[2,4,16,192]{3,2,1,0:T(8,128)(2,1)}, bf16[2,4,16,192]{3,2,1,0:T(8,128)(2,1)S(1)}, u32[]{:S(2)}, u32[]{:S(2)}) collective-permute-start(bf16[2,4,16,192]{3,2,1,0:T(8,128)(2,1)} %get-tuple-element.332), channel_id=1, source_target_pairs={{0,8},{8,16},{16,24},{1,9},{9,17},{17,25},{2,10},{10,18},{18,26},{... | collective-permute-start | bytes 147464 | tf_op jit(solution)/shard_map/ppermute | solution.py:31
  145.2 6.3 %collective-permute-start.32 = (bf16[2,1,16,384]{3,2,1,0:T(8,128)(2,1)S(1)}, bf16[2,1,16,384]{3,2,1,0:T(8,128)(2,1)S(1)}, u32[]{:S(2)}, u32[]{:S(2)}) collective-permute-start(bf16[2,1,16,384]{3,2,1,0:T(8,128)(2,1)S(1)} %get-tuple-element.369), channel_id=1, source_target_pairs={{4,0},{5,1},{6,2},{7,3},{12,8},{13,9},{14,10},{15,11},{20,16},{21,... | collective-permute-start | bytes 73736 | tf_op jit(solution)/shard_map/ppermute | solution.py:15
  146.4 5.1 %collective-permute-start.31 = (bf16[2,1,16,384]{3,2,1,0:T(8,128)(2,1)S(1)}, bf16[2,1,16,384]{3,2,1,0:T(8,128)(2,1)S(1)}, u32[]{:S(2)}, u32[]{:S(2)}) collective-permute-start(bf16[2,1,16,384]{3,2,1,0:T(8,128)(2,1)S(1)} %get-tuple-element.368), channel_id=1, source_target_pairs={{0,4},{1,5},{2,6},{3,7},{8,12},{9,13},{10,14},{11,15},{16,20},{17,... | collective-permute-start | bytes 73736 | tf_op jit(solution)/shard_map/ppermute | solution.py:14
  150.2 7.1 %collective-permute-start.35 = (bf16[2,4,16,192]{3,2,1,0:T(8,128)(2,1)S(1)}, bf16[2,4,16,192]{3,2,1,0:T(8,128)(2,1)S(1)}, u32[]{:S(2)}, u32[]{:S(2)}) collective-permute-start(bf16[2,4,16,192]{3,2,1,0:T(8,128)(2,1)S(1)} %convert_element_type.118), channel_id=1, source_target_pairs={{0,8},{8,16},{16,24},{1,9},{9,17},{17,25},{2,10},{10,18},{18,26},{... | collective-permute-start | bytes 147464 | tf_op jit(solution)/shard_map/ppermute | solution.py:31
  151.7 5.6 %collective-permute-start.34 = (bf16[2,6,1,384]{3,2,1,0:T(2,128)(2,1)S(1)}, bf16[2,6,1,384]{3,2,1,0:T(2,128)(2,1)S(1)}, u32[]{:S(2)}, u32[]{:S(2)}) collective-permute-start(bf16[2,6,1,384]{3,2,1,0:T(2,128)(2,1)S(1)} %get-tuple-element.357), channel_id=1, source_target_pairs={{1,0},{2,1},{3,2},{5,4},{6,5},{7,6},{9,8},{10,9},{11,10},{13,12},{... | collective-permute-start | bytes 27656 | tf_op jit(solution)/shard_map/ppermute | solution.py:15
  153.6 5.7 %collective-permute-start.33 = (bf16[2,6,1,384]{3,2,1,0:T(2,128)(2,1)S(1)}, bf16[2,6,1,384]{3,2,1,0:T(2,128)(2,1)S(1)}, u32[]{:S(2)}, u32[]{:S(2)}) collective-permute-start(bf16[2,6,1,384]{3,2,1,0:T(2,128)(2,1)S(1)} %get-tuple-element.356), channel_id=1, source_target_pairs={{0,1},{1,2},{2,3},{4,5},{5,6},{6,7},{8,9},{9,10},{10,11},{12,13},{... | collective-permute-start | bytes 27656 | tf_op jit(solution)/shard_map/ppermute | solution.py:14
Sparse Core Ops, SparseCore 0:
  8.9 16.4 all-gather.2
where the time goes:
time: 173 us; the launch traced here: 172 us
  waiting for transfers between devices  76.2 us (44%)
  starting transfers between devices  62.3 us (36%)
  between operations  14.3 us (8%)
  other arithmetic  7.34 us (4%)
  matrix products  6.94 us (4%)
  local copies, waits for them, and re-layouts  4.23 us (2%)
    ppermute x12, waiting for transfers between devices, from_behind(): return lax.ppermute(block, axis, route)  57.5 us
    ppermute x12, starting transfers between devices, with_halo(): before = lax.ppermute(last, axis, up)  25.9 us
    ppermute x12, starting transfers between devices, with_halo(): after = lax.ppermute(first, axis, down)  20.9 us
    ppermute x12, starting transfers between devices, from_behind(): return lax.ppermute(block, axis, route)  15.5 us
    ppermute x12, waiting for transfers between devices, with_halo(): before = lax.ppermute(last, axis, up)  13.9 us
    dot_general x2, matrix products, run_step(): jnp.dot(patches_now, layer_weight, preferred_element_type=jnp.float32)  6.94 us
    all_gather x1, waiting for transfers between devices, local(): weight = lax.all_gather(gate_weight[0], 'row', axis=0, tiled=True)  3.87 us
  transfers between devices with their start and end apart: 37, of which 19 were waited for; matrix products, arithmetic and copies ran while one was open for 2% of the time, Pallas kernels for 0%

commit v1 on v0

v1 whole, which is shorter than its diff:
```python
import functools

import jax
import jax.numpy as jnp
from jax import lax
from jax.experimental import pallas as pl
from jax.experimental.pallas import tpu as pltpu
from jax.sharding import PartitionSpec as P

STEPS = 6
HALO = 8
TAPS = 9
BF = jnp.bfloat16
F32 = jnp.float32


def moved(block, axis, pairs):
    return lax.ppermute(block, axis, pairs)


def section_send(block, source, target):
    return lax.ppermute(block, "section", [(source, target)])


def gather_sequence(features):
    batch = features.shape[0]
    size = lax.axis_size("row")
    place = lax.axis_index("row") % batch
    mine = lax.dynamic_index_in_dim(features, place, 0, keepdims=False)
    parts = [mine]
    for k in range(1, batch):
        pairs = [(i, i - i % batch + (i % batch + k) % batch) for i in range(size)]
        sent = lax.dynamic_index_in_dim(features, (place + k) % batch, 0, keepdims=False)
        parts.append(moved(sent, "row", pairs))
    stacked = jnp.stack(parts)
    blocks = [
        lax.dynamic_index_in_dim(stacked, (place - q) % batch, 0, keepdims=False)
        for q in range(batch)
    ]
    return jnp.concatenate(blocks, axis=1)


def with_halo(array, axis, dim, stride):
    size, length = lax.axis_size(axis), array.shape[dim]
    up = [(i, i + stride) for i in range(size - stride)]
    down = [(j, i) for i, j in up]
    last = lax.slice_in_dim(array, length - HALO, length, axis=dim)
    first = lax.slice_in_dim(array, 0, HALO, axis=dim)
    before = moved(last, axis, up)
    after = moved(first, axis, down)
    return jnp.concatenate([before, array, after], axis=dim)


def sigmoid(x):
    return 0.5 * jnp.tanh(0.5 * x) + 0.5


class Step:
    def __init__(self, width, pixels, channels, shards):
        self.width, self.pixels, self.channels, self.shards = (width, pixels, channels, shards)

    def weight_copy(self, ref, wbuf, sems, tap, part):
        rows = self.channels
        dst = wbuf.at[part, pl.ds(tap * rows, rows), :]
        block = (2 * tap + part) % (2 * TAPS // self.shards)
        src = ref.at[pl.ds(block * rows, rows), :]
        return pltpu.make_async_copy(src, dst, sems.at[part, tap])

    def start_weights(self, info, w_refs, wbuf, sems, part):
        for tap in range(TAPS):
            shard = (2 * tap + part) // (2 * TAPS // self.shards)
            for which, ref in enumerate(w_refs):
                owner = lax.rem(info[1] + which, self.shards)

                @pl.when(owner == shard)
                def _():
                    self.weight_copy(ref, wbuf, sems, tap, part).start()

    def wait_weights(self, info, w_refs, wbuf, sems, part, row_tap):
        for tap in range(3 * row_tap, 3 * row_tap + 3):
            self.weight_copy(w_refs[0], wbuf, sems, tap, part).wait()

    def spread(self, value, shift_ref, wide_ref):
        width, pixels, channels = self.width, self.pixels, self.channels
        shift_ref[pl.ds(8, pixels), :] = value.astype(F32)
        for k, offset in enumerate((7, 8, 9)):
            wide_ref[pl.ds(width, pixels), pl.ds(k * channels, channels)] = shift_ref[
                pl.ds(offset, pixels), :
            ].astype(BF)

    def clear(self, shift_ref, wide_ref):
        width, pixels, channels = self.width, self.pixels, self.channels
        shift_ref[pl.ds(0, 8), :] = jnp.zeros((8, channels), F32)
        shift_ref[pl.ds(8 + pixels, 8), :] = jnp.zeros((8, channels), F32)
        wide_ref[pl.ds(0, width), :] = jnp.zeros((width, 3 * channels), BF)
        wide_ref[pl.ds(width + pixels, width), :] = jnp.zeros((width, 3 * channels), BF)

    def product(self, info, w_refs, wbuf, sems, part, wide_ref, wait):
        total = None
        span = 3 * self.channels
        for row_tap in range(3):
            if wait:
                self.wait_weights(info, w_refs, wbuf, sems, part, row_tap)
            term = jnp.dot(
                wide_ref[pl.ds(row_tap * self.width, self.pixels), :],
                wbuf[part, pl.ds(row_tap * span, span), :],
                preferred_element_type=F32,
            )
            total = term if total is None else total + term
        return total

    def update(self, info, gates_ref, bias_ref, memory_ref, hidden_out, memory_out):
        ch = self.channels
        chunk = self.width
        low, high, top, bottom = info[2], info[3], info[4], info[5]

        def body(i, carry):
            rows = pl.ds(pl.multiple_of(i * chunk, chunk), chunk)
            gates = gates_ref[rows, :] + bias_ref[...]
            in_gate = sigmoid(gates[:, :ch])
            candidate = jnp.tanh(gates[:, 2 * ch : 3 * ch])
            memory = in_gate * candidate
            if memory_ref is not None:
                forget = sigmoid(gates[:, ch : 2 * ch])
                memory = memory + forget * memory_ref[rows, :].astype(F32)
            hidden = sigmoid(gates[:, 3 * ch :]) * jnp.tanh(memory)
            column = lax.broadcasted_iota(jnp.int32, hidden.shape, 0)
            inside = (column >= low) & (column < high) & (i >= top) & (i < bottom)
            hidden_out[rows, :] = jnp.where(inside, hidden, 0.0).astype(BF)
            if memory_out is not None:
                memory_out[rows, :] = memory.astype(memory_out.dtype)
            return carry

        lax.fori_loop(0, self.pixels // chunk, body, 0)


def step_call(cfg, turn, info, shards, bias, terms, gates_in=None, memory=None, keep=None, after=None,
              memory_dtype=F32):
    pixels, channels, width = cfg.pixels, cfg.channels, cfg.width
    gate_width = 4 * channels
    arrays = [a for a, _ in terms]
    parts = [p for _, p in terms]
    needed = sorted(set(parts + ([after] if after is not None else [])))
    n_shards, n_terms = len(shards), len(terms)
    has_gates, has_memory = gates_in is not None, memory is not None
    operands = [info, bias] + list(shards) + arrays
    specs = [pl.BlockSpec(memory_space=pltpu.SMEM), pl.BlockSpec(memory_space=pltpu.VMEM)]
    specs += [pl.BlockSpec(memory_space=pl.ANY)] * n_shards
    specs += [pl.BlockSpec(memory_space=pltpu.VMEM)] * n_terms
    if has_gates:
        operands.append(gates_in)
        specs.append(pl.BlockSpec(memory_space=pltpu.VMEM))
    if has_memory:
        operands.append(memory)
        specs.append(pl.BlockSpec(memory_space=pltpu.VMEM))
    outs = [jax.ShapeDtypeStruct((pixels, channels), BF), jax.ShapeDtypeStruct((pixels, channels), memory_dtype)]
    if keep is not None:
        outs.append(jax.ShapeDtypeStruct((pixels, gate_width), F32))
    if after is not None:
        outs.append(jax.ShapeDtypeStruct((pixels, gate_width), F32))

    def kernel(*refs):
        refs = list(refs)
        info_ref, bias_ref = refs.pop(0), refs.pop(0)
        w_refs = [refs.pop(0) for _ in range(n_shards)]
        term_refs = [refs.pop(0) for _ in range(n_terms)]
        gates_ref = refs.pop(0) if has_gates else None
        memory_ref = refs.pop(0) if has_memory else None
        hidden_out, memory_out = refs.pop(0), refs.pop(0)
        keep_out = refs.pop(0) if keep is not None else None
        after_out = refs.pop(0) if after is not None else None
        wbuf, sems, shift_ref, wide_ref, sum_ref = refs

        @pl.when(info_ref[0] == turn)
        def _():
            for part in needed:
                cfg.start_weights(info_ref, w_refs, wbuf, sems, part)
            cfg.clear(shift_ref, wide_ref)
            total = gates_ref[...] if has_gates else None
            waited = set()
            for n, (ref, part) in enumerate(zip(term_refs, parts)):
                if n == 0 or term_refs[n] is not term_refs[n - 1]:
                    cfg.spread(ref[...], shift_ref, wide_ref)
                term = cfg.product(info_ref, w_refs, wbuf, sems, part, wide_ref, part not in waited)
                waited.add(part)
                total = term if total is None else total + term
                if keep == n:
                    keep_out[...] = total
            sum_ref[...] = total
            cfg.update(info_ref, sum_ref, bias_ref, memory_ref, hidden_out, memory_out)
            if after is not None:
                cfg.spread(hidden_out[...], shift_ref, wide_ref)
                after_out[...] = cfg.product(
                    info_ref, w_refs, wbuf, sems, after, wide_ref, after not in waited
                )

    products = n_terms + (after is not None)
    flops = 2 * pixels * TAPS * channels * gate_width * products
    return pl.pallas_call(
        kernel,
        out_shape=outs,
        in_specs=specs,
        out_specs=[pl.BlockSpec(memory_space=pltpu.VMEM)] * len(outs),
        scratch_shapes=[
            pltpu.VMEM((2, TAPS * channels, gate_width), BF),
            pltpu.SemaphoreType.DMA((2, TAPS)),
            pltpu.VMEM((pixels + 16, channels), F32),
            pltpu.VMEM((pixels + 2 * width, 3 * channels), BF),
            pltpu.VMEM((pixels, gate_width), F32),
        ],
        cost_estimate=pl.CostEstimate(
            flops=flops, bytes_accessed=len(needed) * TAPS * channels * gate_width * 2, transcendentals=0
        ),
        compiler_params=pltpu.CompilerParams(vmem_limit_bytes=40 * 1024 * 1024),
        name=f"step{turn}",
    )(*operands)


def local(features, gate_weight, gate_bias):
    batch, frames, tile_rows, tile_cols, channels = features.shape
    section, row, col = (lax.axis_index(a) for a in ("section", "row", "col"))
    row_size, col_size = lax.axis_size("row"), lax.axis_size("col")
    groups = row_size // batch
    place, group = row % batch, row // batch

    own_weight = gate_weight[0]
    if own_weight.shape[0] % channels == 0 and row_size == 2:
        shards = [own_weight, moved(own_weight, "row", [(0, 1), (1, 0)])]
    else:
        shards = [lax.all_gather(own_weight, "row", axis=0, tiled=True)]

    window = gather_sequence(features)
    if groups > 1:
        window = with_halo(window, "row", 1, batch)
    window = with_halo(window, "col", 2, 1)
    height, width = window.shape[1:3]
    pixels = height * width
    window = window.reshape(frames, pixels, channels)

    row_halo = HALO if groups > 1 else 0
    info = jnp.stack(
        [
            section,
            row % len(shards),
            jnp.where(col == 0, HALO, 0),
            jnp.where(col == col_size - 1, width - HALO, width),
            jnp.where(group == 0, row_halo, 0),
            jnp.where(group == groups - 1, height - row_halo, height),
        ]
    ).astype(jnp.int32)

    cfg = Step(width, pixels, channels, len(shards))
    call = functools.partial(step_call, cfg)

    h00, c00 = call(0, info, shards, gate_bias, [(window[0], 0)])
    x10 = section_send(h00, 0, 1)
    h01, c01 = call(0, info, shards, gate_bias, [(window[1], 0), (h00, 1)], memory=c00, memory_dtype=BF)
    x11 = section_send(h01, 0, 1)
    h10, c10, p11 = call(1, info, shards, gate_bias, [(x10, 0)], after=1)
    start3_h = section_send(h01, 0, 3)
    start3_c = section_send(c01, 0, 3)
    h11, c11 = call(1, info, shards, gate_bias, [(x11, 0)], gates_in=p11, memory=c10, memory_dtype=BF)
    x2 = section_send(h11, 1, 2)
    m2 = section_send(c11, 1, 2)
    h20, c20, p21 = call(2, info, shards, gate_bias, [(x2, 0), (x2, 1)], memory=m2, keep=0)
    x30 = section_send(h20, 2, 3)
    h21, _ = call(2, info, shards, gate_bias, [(h20, 1)], gates_in=p21, memory=c20)
    x31 = section_send(h21, 2, 3)
    h30, c30, p31 = call(3, info, shards, gate_bias, [(start3_h, 1), (x30, 0)], memory=start3_c, after=1)
    h31, _ = call(3, info, shards, gate_bias, [(x31, 0)], gates_in=p31, memory=c30)

    def pick(*options):
        return lax.select_n(section, *options)

    result = []
    for options in ((h00, h10, h20, h30), (h01, h11, h21, h31)):
        whole = pick(*options).reshape(height, width, channels)
        inner = whole[row_halo : height - row_halo, HALO : HALO + tile_cols]
        inner = inner.reshape(batch, tile_rows, tile_cols, channels)
        parts = [lax.dynamic_index_in_dim(inner, place, 0, keepdims=False)]
        for k in range(1, batch):
            pairs = [(i, i - i % batch + (i % batch + k) % batch) for i in range(row_size)]
            sent = lax.dynamic_index_in_dim(inner, (place + k) % batch, 0, keepdims=False)
            parts.append(moved(sent, "row", pairs))
        stacked = jnp.stack(parts)
        result.append(
            jnp.stack(
                [
                    lax.dynamic_index_in_dim(stacked, (place - q) % batch, 0, keepdims=False)
                    for q in range(batch)
                ]
            )
        )
    return jnp.stack(result, 1)[None]


def solution(mesh):
    return jax.shard_map(
        local,
        mesh=mesh,
        in_specs=(P(None, None, "row", "col", None), P("section", "row", None), P("section", None)),
        out_specs=P("section", None, None, "row", "col", None),
        check_vma=False,
    )
```

time: 173 us -> 86.3 us (0.50)
  starting transfers between devices: 62.3 us -> 12.9 us
  waiting for transfers between devices: 76.2 us -> 38.1 us
  Pallas kernels: 0 us -> 23.2 us
  between operations: 14.3 us -> 0.45 us
  matrix products: 6.94 us -> 0 us
  other arithmetic: 7.34 us -> 1.02 us
  local copies, waits for them, and re-layouts: 4.23 us -> 9.58 us
    ppermute x36 -> x14, starting transfers between devices: 62.3 us -> 12.9 us  [the longest x8 8.1 us: section_send(): return lax.ppermute(block, 'section', [(source, target)])]
    ppermute x36 -> x14, waiting for transfers between devices: 71.6 us -> 38.1 us  [the longest x8 28.7 us: section_send(): return lax.ppermute(block, 'section', [(source, target)])]
    pallas_call x0 -> x8, Pallas kernels: none -> 23.2 us  [step_call(): pl.pallas_call(kernel, out_shape=outs, in_specs=specs, out_specs=[pl.Bloc...]
    unnamed x2 -> x30, local copies, waits for them, and re-layouts: 0.01 us -> 8.55 us
    dot_general x2 -> x0, matrix products: 6.94 us -> none  [run_step(): jnp.dot(patches_now, layer_weight, preferred_element_type=jnp.float32)]
    all_gather x1 -> x0, waiting for transfers between devices: 3.87 us -> none  [local(): weight = lax.all_gather(gate_weight[0], 'row', axis=0, tiled=True)]
    cond x26 -> x0, local copies, waits for them, and re-layouts: 3.16 us -> none
    concatenate x22 -> x2, other arithmetic: 2.11 us -> 0.06 us  [the longest x1 0.04 us: with_halo(): return jnp.concatenate([before, array, after], axis=dim)]
  transfers between devices with their start and end apart: 37 -> 14, of which waited for: 19 -> 9; matrix products, arithmetic and copies ran while one was open for 2% -> 1% of each run, Pallas kernels for 0% -> 19%
where the time goes in v1:
time: 86.3 us; the launch traced here: 85.3 us
  waiting for transfers between devices  38.1 us (44%)
  Pallas kernels  23.2 us (27%)
  starting transfers between devices  12.9 us (15%)
  local copies, waits for them, and re-layouts  9.58 us (11%)
  other arithmetic  1.02 us (1%)
    ppermute x8, waiting for transfers between devices, section_send(): return lax.ppermute(block, 'section', [(source, target)])  28.7 us
    pallas_call x8, Pallas kernels, step_call(): pl.pallas_call(kernel, out_shape=outs, in_specs=specs, out_specs=[pl.Bloc...  23.2 us
    ppermute x6, waiting for transfers between devices, moved(): return lax.ppermute(block, axis, pairs)  9.43 us
    unnamed x30, local copies, waits for them, and re-layouts  8.55 us
    ppermute x8, starting transfers between devices, section_send(): return lax.ppermute(block, 'section', [(source, target)])  8.1 us
    ppermute x6, starting transfers between devices, moved(): return lax.ppermute(block, axis, pairs)  4.83 us
  transfers between devices with their start and end apart: 14, of which 9 were waited for; matrix products, arithmetic and copies ran while one was open for 1% of the time, Pallas kernels for 19%

profile of v1, /device:TPU:30, one launch (start us, length us, event | category | flops | bytes accessed | tf_op | source)
XLA Modules:
  0.0 85.3 jit_solution(3958560239221098487)
XLA Ops:
  0.0 0.0 collective-permute-start
  0.0 0.9 %dynamic-slice_bitcast_fusion = (bf16[2,4,16,192]{3,2,1,0:T(8,128)(2,1)S(1)}, bf16[1,2,4,16,192]{4,3,2,1,0:T(8,128)(2,1)S(1)}) fusion(bf16[2,2,4,16,192]{4,3,2,1,0:T(8,128)(2,1)} %param.3, s32[]{:T(128)S(6)} %select_n.119, s32[]{:T(128)S(6)} %select_n.117), kind=kLoop, calls=%fused_computation.26 | loop fusion | bytes 196616 | tf_op jit(solution)/shard_map/jit(dynamic_index_in_dim)/squeeze | solution.py:33
  0.9 0.6 collective-permute-start.1
  1.5 3.8 %collective-permute-done.1 = bf16[2,4,16,192]{3,2,1,0:T(8,128)(2,1)S(1)} collective-permute-done((bf16[2,4,16,192]{3,2,1,0:T(8,128)(2,1)S(1)}, bf16[2,4,16,192]{3,2,1,0:T(8,128)(2,1)S(1)}, u32[]{:S(2)}, u32[]{:S(2)}) %collective-permute-start.1) | collective-permute-done | bytes 49184 | tf_op jit(solution)/shard_map/ppermute | solution.py:18
  5.3 0.1 fusion.4
  5.4 2.4 %collective-permute-start.3 = (bf16[2,8,8,192]{3,2,1,0:T(8,128)(2,1)S(1)}, bf16[2,8,8,192]{3,2,1,0:T(8,128)(2,1)S(1)}, u32[]{:S(2)}, u32[]{:S(2)}) collective-permute-start(bf16[2,8,8,192]{3,2,1,0:T(8,128)(2,1)S(1)} %get-tuple-element.42), channel_id=1, source_target_pairs={{1,0},{2,1},{3,2},{5,4},{6,5},{7,6},{9,8},{10,9},{11,10},{13,12},{... | collective-permute-start | bytes 147464 | tf_op jit(solution)/shard_map/ppermute | solution.py:18
  7.7 1.3 %collective-permute-start.2 = (bf16[2,8,8,192]{3,2,1,0:T(8,128)(2,1)S(1)}, bf16[2,8,8,192]{3,2,1,0:T(8,128)(2,1)S(1)}, u32[]{:S(2)}, u32[]{:S(2)}) collective-permute-start(bf16[2,8,8,192]{3,2,1,0:T(8,128)(2,1)S(1)} %get-tuple-element.41), channel_id=1, source_target_pairs={{0,1},{1,2},{2,3},{4,5},{5,6},{6,7},{8,9},{9,10},{10,11},{12,13},{... | collective-permute-start | bytes 147464 | tf_op jit(solution)/shard_map/ppermute | solution.py:18
  9.0 0.1 stack.61.refs_0_
  9.1 0.5 collective-permute-done.3
  9.6 4.3 %collective-permute-done.2 = bf16[2,8,8,192]{3,2,1,0:T(8,128)(2,1)S(1)} collective-permute-done((bf16[2,8,8,192]{3,2,1,0:T(8,128)(2,1)S(1)}, bf16[2,8,8,192]{3,2,1,0:T(8,128)(2,1)S(1)}, u32[]{:S(2)}, u32[]{:S(2)}) %collective-permute-start.2) | collective-permute-done | bytes 49184 | tf_op jit(solution)/shard_map/ppermute | solution.py:18
  14.0 0.0 copy-start
  14.0 2.7 %copy-done = bf16[1,1728,768]{2,1,0:T(8,128)(2,1)S(1)} copy-done((bf16[1,1728,768]{2,1,0:T(8,128)(2,1)S(1)}, bf16[1,1728,768]{2,1,0:T(8,128)(2,1)}, u32[]{:S(2)}) %copy-start) | copy-done | bytes 2654232
  16.7 0.7 copy-done.9
  17.4 0.7 step0.2
  18.1 0.7 collective-permute-start.4
  18.8 1.4 %step0.3 = (bf16[256,192]{1,0:T(8,128)(2,1)}, bf16[256,192]{1,0:T(8,128)(2,1)}) custom-call(s32[6]{0:T(128)S(1)} %stack.61.refs_0_, f32[1,768]{1,0:T(1,128)S(1)} %copy-done.9, bf16[1728,768]{1,0:T(8,128)(2,1)S(1)} %bitcast.32, bf16[1728,768]{1,0:T(8,128)(2,1)S(1)} %collective-permute-done.refs_3_, bf16[256,192]{1,0:T(8,128)(2,1)S(1)} %bitcast.39, ...), custom_call_target="tpu_custom_call" | custom-call | flops 1358954496 | bytes 5308416 | tf_op jit(solution)/shard_map/step0/pallas_call | solution.py:199
  20.2 0.7 collective-permute-start.5
  20.9 0.0 collective-permute-done.4.refs_4_
  20.9 0.7 step1.2
  21.6 0.0 collective-permute-done.5.refs_4_
  21.6 0.7 step1.3
  22.4 0.7 collective-permute-start.6
  23.1 0.7 collective-permute-start.7
  23.7 1.3 %collective-permute-start.8 = (bf16[256,192]{1,0:T(8,128)(2,1)}, bf16[256,192]{1,0:T(8,128)(2,1)}, u32[]{:S(2)}, u32[]{:S(2)}) collective-permute-start(bf16[256,192]{1,0:T(8,128)(2,1)} %get-tuple-element.25), channel_id=1, source_target_pairs={{0,24},{1,25},{2,26},{3,27},{4,28},{5,29},{6,30},{7,31}} | collective-permute-start | bytes 294920 | tf_op jit(solution)/shard_map/ppermute | solution.py:22
  25.0 0.0 copy-start.1
  25.1 1.6 %collective-permute-start.10 = (bf16[256,192]{1,0:T(8,128)(2,1)}, bf16[256,192]{1,0:T(8,128)(2,1)}, u32[]{:S(2)}, u32[]{:S(2)}) collective-permute-start(bf16[256,192]{1,0:T(8,128)(2,1)} %get-tuple-element.31), channel_id=1, source_target_pairs={{0,24},{1,25},{2,26},{3,27},{4,28},{5,29},{6,30},{7,31}} | collective-permute-start | bytes 294920 | tf_op jit(solution)/shard_map/ppermute | solution.py:22
  26.7 1.7 %copy-done.3 = bf16[1728,768]{1,0:T(8,128)(2,1)S(1)} copy-done((bf16[1728,768]{1,0:T(8,128)(2,1)S(1)}, bf16[1728,768]{1,0:T(8,128)(2,1)}, u32[]{:S(2)}) %copy-start.3) | copy-done | bytes 2654232
  28.4 1.6 %step2.2 = (bf16[256,192]{1,0:T(8,128)(2,1)}, f32[256,192]{1,0:T(8,128)S(1)}, f32[256,768]{1,0:T(8,128)S(1)}) custom-call(s32[6]{0:T(128)S(1)} %stack.61.refs_0_, f32[1,768]{1,0:T(1,128)S(1)} %copy-done.9, bf16[1728,768]{1,0:T(8,128)(2,1)S(1)} %bitcast.35, bf16[1728,768]{1,0:T(8,128)(2,1)S(1)} %copy-done.3, ...), custom_call_target="tpu_custom_call" | custom-call | flops 1358954496 | bytes 5308416 | tf_op jit(solution)/shard_map/step2/pallas_call | solution.py:199
  30.0 0.7 copy-done.7
  30.7 1.3 %collective-permute-start.9 = (bf16[256,192]{1,0:T(8,128)(2,1)}, bf16[256,192]{1,0:T(8,128)(2,1)}, u32[]{:S(2)}, u32[]{:S(2)}) collective-permute-start(bf16[256,192]{1,0:T(8,128)(2,1)} %get-tuple-element.30.refs_4_), channel_id=1, source_target_pairs={{16,24},{17,25},{18,26},{19,27},{20,28},{21,29},{22,30},{23,31}} | collective-permute-start | bytes 294920 | tf_op jit(solution)/shard_map/ppermute | solution.py:22
  32.0 1.7 %copy-done.4 = bf16[1728,768]{1,0:T(8,128)(2,1)S(1)} copy-done((bf16[1728,768]{1,0:T(8,128)(2,1)S(1)}, bf16[1728,768]{1,0:T(8,128)(2,1)}, u32[]{:S(2)}) %copy-start.4) | copy-done | bytes 2654232
  33.8 0.9 %copy-done.8 = f32[256,192]{1,0:T(8,128)S(1)} copy-done((f32[256,192]{1,0:T(8,128)S(1)}, f32[256,192]{1,0:T(8,128)}, u32[]{:S(2)}) %copy-start.8) | copy-done | bytes 196632
  34.7 1.8 %step2.3 = (bf16[256,192]{1,0:T(8,128)(2,1)S(1)}, f32[256,192]{1,0:T(8,128)}) custom-call(s32[6]{0:T(128)S(1)} %stack.61.refs_0_, f32[1,768]{1,0:T(1,128)S(1)} %copy-done.10, bf16[1728,768]{1,0:T(8,128)(2,1)S(1)} %bitcast.36, bf16[1728,768]{1,0:T(8,128)(2,1)S(1)} %copy-done.4, bf16[256,192]{1,0:T(8,128)(2,1)} %get-tuple-element.30.refs_4_, ...), custom_call_target="tpu_custom_call" | custom-call | flops 679477248 | bytes 2654208 | tf_op jit(solution)/shard_map/step2/pallas_call | solution.py:199
  36.5 1.3 %collective-permute-start.12 = (bf16[256,192]{1,0:T(8,128)(2,1)S(1)}, bf16[256,192]{1,0:T(8,128)(2,1)S(1)}, u32[]{:S(2)}, u32[]{:S(2)}) collective-permute-start(bf16[256,192]{1,0:T(8,128)(2,1)S(1)} %get-tuple-element.35), channel_id=1, source_target_pairs={{16,24},{17,25},{18,26},{19,27},{20,28},{21,29},{22,30},{23,31}} | collective-permute-start | bytes 294920 | tf_op jit(solution)/shard_map/ppermute | solution.py:22
  37.8 6.0 %collective-permute-done.8.refs_4_ = bf16[256,192]{1,0:T(8,128)(2,1)} collective-permute-done((bf16[256,192]{1,0:T(8,128)(2,1)}, bf16[256,192]{1,0:T(8,128)(2,1)}, u32[]{:S(2)}, u32[]{:S(2)}) %collective-permute-start.8) | collective-permute-done | bytes 98336 | tf_op jit(solution)/shard_map/ppermute | solution.py:22
  43.8 1.4 %collective-permute-done.10.refs_6_ = bf16[256,192]{1,0:T(8,128)(2,1)} collective-permute-done((bf16[256,192]{1,0:T(8,128)(2,1)}, bf16[256,192]{1,0:T(8,128)(2,1)}, u32[]{:S(2)}, u32[]{:S(2)}) %collective-permute-start.10) | collective-permute-done | bytes 98336 | tf_op jit(solution)/shard_map/ppermute | solution.py:22
  45.2 20.9 %collective-permute-done.9.refs_5_ = bf16[256,192]{1,0:T(8,128)(2,1)} collective-permute-done((bf16[256,192]{1,0:T(8,128)(2,1)}, bf16[256,192]{1,0:T(8,128)(2,1)}, u32[]{:S(2)}, u32[]{:S(2)}) %collective-permute-start.9) | collective-permute-done | bytes 98336 | tf_op jit(solution)/shard_map/ppermute | solution.py:22
  66.1 10.3 %step3.2 = (bf16[256,192]{1,0:T(8,128)(2,1)S(1)}, f32[256,192]{1,0:T(8,128)S(1)}, f32[256,768]{1,0:T(8,128)S(1)}) custom-call(s32[6]{0:T(128)S(1)} %stack.61.refs_0_, f32[1,768]{1,0:T(1,128)S(1)} %copy-done.10, bf16[1728,768]{1,0:T(8,128)(2,1)S(1)} %bitcast.37, bf16[1728,768]{1,0:T(8,128)(2,1)S(1)} %copy-done.4, ...), custom_call_target="tpu_custom_call" | custom-call | flops 2038431744 | bytes 5308416 | tf_op jit(solution)/shard_map/step3/pallas_call | solution.py:199
  76.4 0.4 collective-permute-done.12.refs_4_
  76.8 6.0 %step3.3 = (bf16[256,192]{1,0:T(8,128)(2,1)S(1)}, f32[256,192]{1,0:T(8,128)}) custom-call(s32[6]{0:T(128)S(1)} %stack.61.refs_0_, f32[1,768]{1,0:T(1,128)S(1)} %copy-done.10, bf16[1728,768]{1,0:T(8,128)(2,1)S(1)} %bitcast.38, bf16[1728,768]{1,0:T(8,128)(2,1)S(1)} %copy-done.4, bf16[256,192]{1,0:T(8,128)(2,1)S(1)} %collective-permute-done.12.refs_4_, ...), custom_call_target="tpu_custom_call" | custom-call | flops 679477248 | bytes 2654208 | tf_op jit(solution)/shard_map/step3/pallas_call | solution.py:199
  82.8 0.1 select_select_fusion
  82.9 0.1 collective-permute-start.13
  83.0 0.1 select_select_fusion.1
  83.1 0.5 collective-permute-start.11
  83.6 0.5 collective-permute-done.13
  84.1 0.3 collective-permute-done.11
  84.5 0.1 fusion.6
  84.6 0.7 maximum_bitcast_fusion
  (34 shorter events, 0.2 us)
Async XLA Ops:
  0.0 14.0 %collective-permute-start = (bf16[1728,768]{1,0:T(8,128)(2,1)}, bf16[1728,768]{1,0:T(8,128)(2,1)S(1)}, u32[]{:S(2)}, u32[]{:S(2)}) collective-permute-start(bf16[1728,768]{1,0:T(8,128)(2,1)} %bitcast.30), channel_id=1, source_target_pairs={{0,4},{4,0},{1,5},{5,1},{2,6},{6,2},{3,7},{7,3},{8,12},{12,8},{9,1... | collective-permute-start | bytes 7962632 | tf_op jit(solution)/shard_map/ppermute | solution.py:18
  0.9 4.4 %collective-permute-start.1 = (bf16[2,4,16,192]{3,2,1,0:T(8,128)(2,1)S(1)}, bf16[2,4,16,192]{3,2,1,0:T(8,128)(2,1)S(1)}, u32[]{:S(2)}, u32[]{:S(2)}) collective-permute-start(bf16[2,4,16,192]{3,2,1,0:T(8,128)(2,1)S(1)} %get-tuple-element.45), channel_id=1, source_target_pairs={{0,4},{4,0},{1,5},{5,1},{2,6},{6,2},{3,7},{7,3},{8,12},{12,8},{9,1... | collective-permute-start | bytes 147464 | tf_op jit(solution)/shard_map/ppermute | solution.py:18
  5.4 4.2 %collective-permute-start.3 = (bf16[2,8,8,192]{3,2,1,0:T(8,128)(2,1)S(1)}, bf16[2,8,8,192]{3,2,1,0:T(8,128)(2,1)S(1)}, u32[]{:S(2)}, u32[]{:S(2)}) collective-permute-start(bf16[2,8,8,192]{3,2,1,0:T(8,128)(2,1)S(1)} %get-tuple-element.42), channel_id=1, source_target_pairs={{1,0},{2,1},{3,2},{5,4},{6,5},{7,6},{9,8},{10,9},{11,10},{13,12},{... | collective-permute-start | bytes 147464 | tf_op jit(solution)/shard_map/ppermute | solution.py:18
  7.7 6.2 %collective-permute-start.2 = (bf16[2,8,8,192]{3,2,1,0:T(8,128)(2,1)S(1)}, bf16[2,8,8,192]{3,2,1,0:T(8,128)(2,1)S(1)}, u32[]{:S(2)}, u32[]{:S(2)}) collective-permute-start(bf16[2,8,8,192]{3,2,1,0:T(8,128)(2,1)S(1)} %get-tuple-element.41), channel_id=1, source_target_pairs={{0,1},{1,2},{2,3},{4,5},{5,6},{6,7},{8,9},{9,10},{10,11},{12,13},{... | collective-permute-start | bytes 147464 | tf_op jit(solution)/shard_map/ppermute | solution.py:18
  14.0 7.7 %copy-start.2 = (bf16[1728,768]{1,0:T(8,128)(2,1)}, bf16[1728,768]{1,0:T(8,128)(2,1)S(1)}, u32[]{:S(2)}) copy-start(bf16[1728,768]{1,0:T(8,128)(2,1)S(1)} %collective-permute-done.refs_3_) | copy-start | bytes 7962628
  14.0 2.7 %copy-start = (bf16[1,1728,768]{2,1,0:T(8,128)(2,1)S(1)}, bf16[1,1728,768]{2,1,0:T(8,128)(2,1)}, u32[]{:S(2)}) copy-start(bf16[1,1728,768]{2,1,0:T(8,128)(2,1)} %param.4) | copy-start | bytes 7962628
  16.7 0.7 copy-start.9
  18.1 2.1 %copy-start.5 = (bf16[256,192]{1,0:T(8,128)(2,1)}, bf16[256,192]{1,0:T(8,128)(2,1)S(1)}, u32[]{:S(2)}) copy-start(bf16[256,192]{1,0:T(8,128)(2,1)S(1)} %get-tuple-element.22.refs_5_) | copy-start | bytes 294916
  18.1 2.8 %collective-permute-start.4 = (bf16[256,192]{1,0:T(8,128)(2,1)S(1)}, bf16[256,192]{1,0:T(8,128)(2,1)S(1)}, u32[]{:S(2)}, u32[]{:S(2)}) collective-permute-start(bf16[256,192]{1,0:T(8,128)(2,1)S(1)} %get-tuple-element.22.refs_5_), channel_id=1, source_target_pairs={{0,8},{1,9},{2,10},{3,11},{4,12},{5,13},{6,14},{7,15}} | collective-permute-start | bytes 294920 | tf_op jit(solution)/shard_map/ppermute | solution.py:22
  20.2 1.4 %collective-permute-start.5 = (bf16[256,192]{1,0:T(8,128)(2,1)}, bf16[256,192]{1,0:T(8,128)(2,1)S(1)}, u32[]{:S(2)}, u32[]{:S(2)}) collective-permute-start(bf16[256,192]{1,0:T(8,128)(2,1)} %get-tuple-element.25), channel_id=1, source_target_pairs={{0,8},{1,9},{2,10},{3,11},{4,12},{5,13},{6,14},{7,15}} | collective-permute-start | bytes 294920 | tf_op jit(solution)/shard_map/ppermute | solution.py:22
  21.6 0.8 copy-start.11
  22.4 4.3 %copy-start.13 = (bf16[256,192]{1,0:T(8,128)(2,1)}, bf16[256,192]{1,0:T(8,128)(2,1)S(1)}, u32[]{:S(2)}) copy-start(bf16[256,192]{1,0:T(8,128)(2,1)S(1)} %get-tuple-element.28) | copy-start | bytes 294916
  22.4 4.2 %collective-permute-start.6 = (bf16[256,192]{1,0:T(8,128)(2,1)S(1)}, bf16[256,192]{1,0:T(8,128)(2,1)S(1)}, u32[]{:S(2)}, u32[]{:S(2)}) collective-permute-start(bf16[256,192]{1,0:T(8,128)(2,1)S(1)} %get-tuple-element.28), channel_id=1, source_target_pairs={{8,16},{9,17},{10,18},{11,19},{12,20},{13,21},{14,22},{15,23}} | collective-permute-start | bytes 294920 | tf_op jit(solution)/shard_map/ppermute | solution.py:22
  23.1 3.6 %collective-permute-start.7 = (bf16[256,192]{1,0:T(8,128)(2,1)S(1)}, bf16[256,192]{1,0:T(8,128)(2,1)S(1)}, u32[]{:S(2)}, u32[]{:S(2)}) collective-permute-start(bf16[256,192]{1,0:T(8,128)(2,1)S(1)} %get-tuple-element.29), channel_id=1, source_target_pairs={{8,16},{9,17},{10,18},{11,19},{12,20},{13,21},{14,22},{15,23}} | collective-permute-start | bytes 294920 | tf_op jit(solution)/shard_map/ppermute | solution.py:22
  23.7 20.0 %collective-permute-start.8 = (bf16[256,192]{1,0:T(8,128)(2,1)}, bf16[256,192]{1,0:T(8,128)(2,1)}, u32[]{:S(2)}, u32[]{:S(2)}) collective-permute-start(bf16[256,192]{1,0:T(8,128)(2,1)} %get-tuple-element.25), channel_id=1, source_target_pairs={{0,24},{1,25},{2,26},{3,27},{4,28},{5,29},{6,30},{7,31}} | collective-permute-start | bytes 294920 | tf_op jit(solution)/shard_map/ppermute | solution.py:22
  25.0 6.9 %copy-start.1 = (bf16[1,1728,768]{2,1,0:T(8,128)(2,1)S(1)}, bf16[1,1728,768]{2,1,0:T(8,128)(2,1)}, u32[]{:S(2)}) copy-start(bf16[1,1728,768]{2,1,0:T(8,128)(2,1)} %param.4) | copy-start | bytes 7962628
  25.1 20.1 %collective-permute-start.10 = (bf16[256,192]{1,0:T(8,128)(2,1)}, bf16[256,192]{1,0:T(8,128)(2,1)}, u32[]{:S(2)}, u32[]{:S(2)}) collective-permute-start(bf16[256,192]{1,0:T(8,128)(2,1)} %get-tuple-element.31), channel_id=1, source_target_pairs={{0,24},{1,25},{2,26},{3,27},{4,28},{5,29},{6,30},{7,31}} | collective-permute-start | bytes 294920 | tf_op jit(solution)/shard_map/ppermute | solution.py:22
  26.6 1.8 %copy-start.3 = (bf16[1728,768]{1,0:T(8,128)(2,1)S(1)}, bf16[1728,768]{1,0:T(8,128)(2,1)}, u32[]{:S(2)}) copy-start(bf16[1728,768]{1,0:T(8,128)(2,1)} %copy-done.2) | copy-start | bytes 7962628
  28.4 3.6 %copy-start.10 = (f32[1,768]{1,0:T(1,128)S(1)}, f32[1,768]{1,0:T(1,128)}, u32[]{:S(2)}) copy-start(f32[1,768]{1,0:T(1,128)} %refs_1_.15) | copy-start | bytes 9220
  30.0 0.7 copy-start.7
  30.7 35.4 %collective-permute-start.9 = (bf16[256,192]{1,0:T(8,128)(2,1)}, bf16[256,192]{1,0:T(8,128)(2,1)}, u32[]{:S(2)}, u32[]{:S(2)}) collective-permute-start(bf16[256,192]{1,0:T(8,128)(2,1)} %get-tuple-element.30.refs_4_), channel_id=1, source_target_pairs={{16,24},{17,25},{18,26},{19,27},{20,28},{21,29},{22,30},{23,31}} | collective-permute-start | bytes 294920 | tf_op jit(solution)/shard_map/ppermute | solution.py:22
  32.0 1.8 %copy-start.4 = (bf16[1728,768]{1,0:T(8,128)(2,1)S(1)}, bf16[1728,768]{1,0:T(8,128)(2,1)}, u32[]{:S(2)}) copy-start(bf16[1728,768]{1,0:T(8,128)(2,1)} %copy-done.2) | copy-start | bytes 7962628
  33.8 0.9 %copy-start.8 = (f32[256,192]{1,0:T(8,128)S(1)}, f32[256,192]{1,0:T(8,128)}, u32[]{:S(2)}) copy-start(f32[256,192]{1,0:T(8,128)} %copy-done.7) | copy-start | bytes 589828
  36.5 40.3 %collective-permute-start.12 = (bf16[256,192]{1,0:T(8,128)(2,1)S(1)}, bf16[256,192]{1,0:T(8,128)(2,1)S(1)}, u32[]{:S(2)}, u32[]{:S(2)}) collective-permute-start(bf16[256,192]{1,0:T(8,128)(2,1)S(1)} %get-tuple-element.35), channel_id=1, source_target_pairs={{16,24},{17,25},{18,26},{19,27},{20,28},{21,29},{22,30},{23,31}} | collective-permute-start | bytes 294920 | tf_op jit(solution)/shard_map/ppermute | solution.py:22
  76.8 6.0 %copy-start.14 = (bf16[256,192]{1,0:T(8,128)(2,1)S(1)}, bf16[256,192]{1,0:T(8,128)(2,1)}, u32[]{:S(2)}) copy-start(bf16[256,192]{1,0:T(8,128)(2,1)} %copy-done.13) | copy-start | bytes 294916
  76.8 6.2 %copy-start.6 = (bf16[256,192]{1,0:T(8,128)(2,1)S(1)}, bf16[256,192]{1,0:T(8,128)(2,1)}, u32[]{:S(2)}) copy-start(bf16[256,192]{1,0:T(8,128)(2,1)} %copy-done.5) | copy-start | bytes 294916
  76.8 6.2 %copy-start.12 = (bf16[256,192]{1,0:T(8,128)(2,1)S(1)}, bf16[256,192]{1,0:T(8,128)(2,1)}, u32[]{:S(2)}) copy-start(bf16[256,192]{1,0:T(8,128)(2,1)} %copy-done.11) | copy-start | bytes 294916
  82.9 1.3 %collective-permute-start.13 = (bf16[4,16,192]{2,1,0:T(8,128)(2,1)S(1)}, bf16[4,16,192]{2,1,0:T(8,128)(2,1)S(1)}, u32[]{:S(2)}, u32[]{:S(2)}) collective-permute-start(bf16[4,16,192]{2,1,0:T(8,128)(2,1)S(1)} %get-tuple-element.53), channel_id=1, source_target_pairs={{0,4},{4,0},{1,5},{5,1},{2,6},{6,2},{3,7},{7,3},{8,12},{12,8},{9,1... | collective-permute-start | bytes 73736 | tf_op jit(solution)/shard_map/ppermute | solution.py:18
  83.1 1.4 %collective-permute-start.11 = (bf16[4,16,192]{2,1,0:T(8,128)(2,1)S(1)}, bf16[4,16,192]{2,1,0:T(8,128)(2,1)S(1)}, u32[]{:S(2)}, u32[]{:S(2)}) collective-permute-start(bf16[4,16,192]{2,1,0:T(8,128)(2,1)S(1)} %get-tuple-element.49), channel_id=1, source_target_pairs={{0,4},{4,0},{1,5},{5,1},{2,6},{6,2},{3,7},{7,3},{8,12},{12,8},{9,1... | collective-permute-start | bytes 73736 | tf_op jit(solution)/shard_map/ppermute | solution.py:18
